TPU v7x, 32 devices: a whole 2x2x4 slice. The times are simulated.
32 devices in a mesh: sub: 8 (over z, y), blk: 4 (over x, core).
Axes of the slice: x: 2, y: 2, z: 4, core: 2. Of those that a mesh axis runs over, the one named last changes fastest.
Arguments:
- initial_state: float32 [8, 64, 2048], P('sub', None, 'blk'), may hold values from -6 to 6
- source: bfloat16 [8, 8, 64, 2048], P('sub', None, None, 'blk'), may hold values from -6 to 6
- inverse_diag: float32 [8, 2048], P('sub', 'blk'), may hold values from 0.5 to 0.85
- inverse_off: bfloat16 [8, 2048, 2048], P('sub', None, 'blk'), may hold values from -0.032958984 to 0.032958984
- coupling: float32 [8, 128], P('sub', 'blk'), may hold values from 0.3 to 3
- initial_waves: bfloat16 [8, 128, 512], P('sub', 'blk'), may hold values from -6 to 6
- bucket: int32 [8], P('sub'), may hold values from 0 to 2
- partner: int32 [8, 128], P('sub', 'blk'), may hold values from 0 to 7
- position_of: int32 [8], replicated, may hold values from 0 to 7, each once
Outputs:
- last_state: float32 [8, 64, 2048], P('sub', None, 'blk')
- waveform: float32 [8, 128, 512], P('sub', 'blk')
Inputs may be any that keep to these rules, and one draw needn't show every extreme that they name: A subcircuit of bucket b takes 8 / 2 ** (2 - b) implicit Euler steps. `position_of`: a permutation.
All inputs are finite; a program needn't handle non-finite values.
Results may differ from a plain program's by a relative error of at most 0.0052.
Values may be sent and summed in bfloat16 or wider, within the bound.
A program may use at most 64 MiB of HBM per device.

v0:
```python
import jax
import jax.numpy as jnp
from jax import lax
from jax.sharding import PartitionSpec as P

SWEEPS = 2


def step_count(bucket, refined_points):
    return jnp.where(
        bucket == 0,
        refined_points // 4,
        jnp.where(bucket == 1, refined_points // 2, refined_points),
    ).astype(jnp.int32)


def port_fetch(waves, selector):
    return jnp.einsum(
        "qjr,rjc->qjc",
        selector,
        lax.all_gather(waves, "sub", axis=0, tiled=True),
        preferred_element_type=jnp.float32,
    ).astype(jnp.bfloat16)


def spread_ports(injected, stride):
    padded = jnp.pad(injected[..., None], [(0, 0)] * injected.ndim + [(0, stride - 1)])
    return padded.reshape(injected.shape[:-1] + (injected.shape[-1] * stride,))


def run_together(
    initial_state, source, inverse_diag, inverse_off, coupling, step_total, spacing, incoming
):
    sub_dev, corners, node_block = initial_state.shape
    refined_points = source.shape[1]
    ports_block = coupling.shape[1]
    stride = node_block // ports_block
    spacing_float = spacing.astype(jnp.float32)
    driven = incoming.astype(jnp.float32).reshape(sub_dev, ports_block, refined_points, corners)
    points = jnp.arange(refined_points, dtype=jnp.int32)

    def contract(totals, shard_rows):
        return totals + jnp.einsum(
            "qcn,qnm->qcm", shard_rows, inverse_off, preferred_element_type=jnp.float32
        )

    def advance(time_step_index, carried):
        current, sample_times = carried
        fine_index = (time_step_index + 1) * spacing - 1
        chosen = points[None, :] == fine_index[:, None]
        forcing = jnp.einsum(
            "qf,qfcn->qcn", chosen.astype(jnp.bfloat16), source, preferred_element_type=jnp.float32
        )
        injected = coupling[:, :, None] * jnp.einsum(
            "qf,qjfc->qjc", chosen.astype(jnp.float32), driven, precision=lax.Precision.HIGHEST
        )
        spread = spread_ports(jnp.swapaxes(injected, 1, 2), stride)
        loop_argument = (current + spacing_float[:, None, None] * (forcing + spread)).astype(
            jnp.bfloat16
        )
        loop_argument = lax.optimization_barrier(loop_argument)
        diagonal_term = inverse_diag[:, None, :] * loop_argument.astype(jnp.float32)
        updated = contract(diagonal_term, lax.all_gather(loop_argument, "blk", axis=2, tiled=True))
        active = time_step_index < step_total
        updated = jnp.where(active[:, None, None], updated, current)
        port_values = updated.reshape(sub_dev, corners, ports_block, stride)[:, :, :, 0]
        sample_times = lax.dynamic_update_index_in_dim(
            sample_times, port_values, time_step_index, 1
        )
        return (updated, sample_times)

    sample_times = jnp.zeros((sub_dev, refined_points, corners, ports_block), jnp.float32)
    last_state, sample_times = lax.fori_loop(
        0, refined_points, advance, (initial_state, sample_times)
    )
    kept_values = (points[None, :, None] // spacing[:, None, None] == points[None, None, :]).astype(
        jnp.float32
    )
    waveform = jnp.einsum(
        "qfk,qkcp->qpfc", kept_values, sample_times, precision=lax.Precision.HIGHEST
    )
    return (last_state, waveform.reshape(sub_dev, ports_block, refined_points * corners))


def shards(
    initial_state,
    source,
    inverse_diag,
    inverse_off,
    coupling,
    initial_waves,
    bucket,
    partner,
    position_of,
):
    refined_points = source.shape[1]
    subs_all = position_of.shape[0]
    identities = jnp.arange(subs_all, dtype=jnp.int32)
    located = jnp.sum(
        jnp.where(partner[:, :, None] == identities[None, None, :], position_of[None, None, :], 0),
        axis=2,
    )
    selector = (located[:, :, None] == identities[None, None, :]).astype(jnp.bfloat16)
    step_total = step_count(bucket, refined_points)
    spacing = refined_points // step_total
    waves = initial_waves
    for sweep_index in range(SWEEPS):
        incoming = port_fetch(waves, selector)
        last_state, waveform = run_together(
            initial_state,
            source,
            inverse_diag,
            inverse_off,
            coupling,
            step_total,
            spacing,
            incoming,
        )
        waves = waveform.astype(jnp.bfloat16)
    return (last_state, waveform)


def solution(mesh):
    return jax.shard_map(
        shards,
        mesh=mesh,
        in_specs=(
            P("sub", None, "blk"),
            P("sub", None, None, "blk"),
            P("sub", "blk"),
            P("sub", None, "blk"),
            P("sub", "blk"),
            P("sub", "blk", None),
            P("sub"),
            P("sub", "blk"),
            P(),
        ),
        out_specs=(P("sub", None, "blk"), P("sub", "blk", None)),
        check_vma=False,
    )
```

profile of v0, /device:TPU:0, one launch (start us, length us, event | category | flops | bytes accessed | tf_op | source)
XLA Modules:
  0.0 216.6 jit_solution(17633719554943924317)
XLA Ops:
  0.6 0.9 copy.118
  3.0 32.8 %all_gather.26 = bf16[8,32,512]{2,1,0:T(8,128)(2,1)S(1)} all-gather(bf16[1,32,512]{2,1,0:T(8,128)(2,1)} %param.20), channel_id=1, replica_groups=mesh['sub'=8,'blk'=4] {'sub'}, dimensions={0}, use_global_device_ids=true | all-gather | bytes 294912 | tf_op jit(solution)/shard_map/all_gather | solution.py:21
  36.2 73.8 %while.36 = (s32[]{:T(128)}, f32[1,64,512]{2,1,0:T(8,128)S(1)}, f32[1,8,64,32]{2,3,1,0:T(8,128)S(1)}, s32[1]{0:T(128)}, f32[1,512]{1,0:T(1,128)}, /*index=5*/f32...) while((s32[]{:T(128)}, f32[1,64,512]{2,1,0:T(8,128)S(1)}, ...), condition=%wide.region_2.3_spmd.clone, body=%wide.region_1.2_spmd.clone.sunk | while | flops 135202832 | bytes 13330811 | solution.py:73
  36.5 0.8 broadcast_multiply_fusion.4
  37.4 1.4 fusion.101
  38.9 5.8 %all_gather.32 = bf16[1,64,2048]{2,1,0:T(8,128)(2,1)S(1)} all-gather(bf16[1,64,512]{2,1,0:T(8,128)(2,1)S(1)} %fusion.102), channel_id=1, replica_groups=mesh['sub'=8,'blk'=4] {'blk'}, dimensions={2}, use_global_device_ids=true | all-gather | bytes 327680 | tf_op jit(solution)/shard_map/while/body/eval_jaxpr/all_gather | solution.py:63
  45.6 0.8 broadcast_multiply_fusion.4
  46.6 1.4 fusion.101
  48.1 5.9 %all_gather.32 = bf16[1,64,2048]{2,1,0:T(8,128)(2,1)S(1)} all-gather(bf16[1,64,512]{2,1,0:T(8,128)(2,1)S(1)} %fusion.102), channel_id=1, replica_groups=mesh['sub'=8,'blk'=4] {'blk'}, dimensions={2}, use_global_device_ids=true | all-gather | bytes 327680 | tf_op jit(solution)/shard_map/while/body/eval_jaxpr/all_gather | solution.py:63
  55.8 1.4 fusion.101
  57.3 5.9 %all_gather.32 = bf16[1,64,2048]{2,1,0:T(8,128)(2,1)S(1)} all-gather(bf16[1,64,512]{2,1,0:T(8,128)(2,1)S(1)} %fusion.102), channel_id=1, replica_groups=mesh['sub'=8,'blk'=4] {'blk'}, dimensions={2}, use_global_device_ids=true | all-gather | bytes 327680 | tf_op jit(solution)/shard_map/while/body/eval_jaxpr/all_gather | solution.py:63
  64.1 0.8 broadcast_multiply_fusion.4
  65.1 1.4 fusion.101
  66.6 5.9 %all_gather.32 = bf16[1,64,2048]{2,1,0:T(8,128)(2,1)S(1)} all-gather(bf16[1,64,512]{2,1,0:T(8,128)(2,1)S(1)} %fusion.102), channel_id=1, replica_groups=mesh['sub'=8,'blk'=4] {'blk'}, dimensions={2}, use_global_device_ids=true | all-gather | bytes 327680 | tf_op jit(solution)/shard_map/while/body/eval_jaxpr/all_gather | solution.py:63
  74.3 1.4 fusion.101
  75.8 5.9 %all_gather.32 = bf16[1,64,2048]{2,1,0:T(8,128)(2,1)S(1)} all-gather(bf16[1,64,512]{2,1,0:T(8,128)(2,1)S(1)} %fusion.102), channel_id=1, replica_groups=mesh['sub'=8,'blk'=4] {'blk'}, dimensions={2}, use_global_device_ids=true | all-gather | bytes 327680 | tf_op jit(solution)/shard_map/while/body/eval_jaxpr/all_gather | solution.py:63
  83.5 1.4 fusion.101
  85.0 5.9 %all_gather.32 = bf16[1,64,2048]{2,1,0:T(8,128)(2,1)S(1)} all-gather(bf16[1,64,512]{2,1,0:T(8,128)(2,1)S(1)} %fusion.102), channel_id=1, replica_groups=mesh['sub'=8,'blk'=4] {'blk'}, dimensions={2}, use_global_device_ids=true | all-gather | bytes 327680 | tf_op jit(solution)/shard_map/while/body/eval_jaxpr/all_gather | solution.py:63
  92.8 1.4 fusion.101
  94.3 5.9 %all_gather.32 = bf16[1,64,2048]{2,1,0:T(8,128)(2,1)S(1)} all-gather(bf16[1,64,512]{2,1,0:T(8,128)(2,1)S(1)} %fusion.102), channel_id=1, replica_groups=mesh['sub'=8,'blk'=4] {'blk'}, dimensions={2}, use_global_device_ids=true | all-gather | bytes 327680 | tf_op jit(solution)/shard_map/while/body/eval_jaxpr/all_gather | solution.py:63
  102.0 1.4 fusion.101
  103.5 5.9 %all_gather.32 = bf16[1,64,2048]{2,1,0:T(8,128)(2,1)S(1)} all-gather(bf16[1,64,512]{2,1,0:T(8,128)(2,1)S(1)} %fusion.102), channel_id=1, replica_groups=mesh['sub'=8,'blk'=4] {'blk'}, dimensions={2}, use_global_device_ids=true | all-gather | bytes 327680 | tf_op jit(solution)/shard_map/while/body/eval_jaxpr/all_gather | solution.py:63
  110.5 30.8 %all_gather.27 = bf16[8,32,512]{2,1,0:T(8,128)(2,1)S(1)} all-gather(bf16[1,32,512]{2,1,0:T(8,128)(2,1)S(1)} %convert_element_type.111), channel_id=1, replica_groups=mesh['sub'=8,'blk'=4] {'sub'}, dimensions={0}, use_global_device_ids=true | all-gather | bytes 294912 | tf_op jit(solution)/shard_map/all_gather | solution.py:21
  141.7 73.8 %while.37 = (s32[]{:T(128)}, f32[1,64,512]{2,1,0:T(8,128)S(1)}, f32[1,8,64,32]{2,3,1,0:T(8,128)S(1)}, s32[1]{0:T(128)}, f32[1,512]{1,0:T(1,128)}, /*index=5*/f32...) while((s32[]{:T(128)}, f32[1,64,512]{2,1,0:T(8,128)S(1)}, ...), condition=%wide.region_4.6_spmd.clone, body=%wide.region_3.5_spmd.clone.sunk | while | flops 135202832 | bytes 13330811 | solution.py:73
  142.0 0.8 broadcast_multiply_fusion.5
  143.0 1.4 fusion.111
  144.5 5.8 %all_gather.33 = bf16[1,64,2048]{2,1,0:T(8,128)(2,1)S(1)} all-gather(bf16[1,64,512]{2,1,0:T(8,128)(2,1)S(1)} %fusion.112), channel_id=1, replica_groups=mesh['sub'=8,'blk'=4] {'blk'}, dimensions={2}, use_global_device_ids=true | all-gather | bytes 327680 | tf_op jit(solution)/shard_map/while/body/eval_jaxpr/all_gather | solution.py:63
  151.1 0.8 broadcast_multiply_fusion.5
  152.1 1.4 fusion.111
  153.6 5.9 %all_gather.33 = bf16[1,64,2048]{2,1,0:T(8,128)(2,1)S(1)} all-gather(bf16[1,64,512]{2,1,0:T(8,128)(2,1)S(1)} %fusion.112), channel_id=1, replica_groups=mesh['sub'=8,'blk'=4] {'blk'}, dimensions={2}, use_global_device_ids=true | all-gather | bytes 327680 | tf_op jit(solution)/shard_map/while/body/eval_jaxpr/all_gather | solution.py:63
  160.4 0.8 broadcast_multiply_fusion.5
  161.4 1.4 fusion.111
  162.9 5.9 %all_gather.33 = bf16[1,64,2048]{2,1,0:T(8,128)(2,1)S(1)} all-gather(bf16[1,64,512]{2,1,0:T(8,128)(2,1)S(1)} %fusion.112), channel_id=1, replica_groups=mesh['sub'=8,'blk'=4] {'blk'}, dimensions={2}, use_global_device_ids=true | all-gather | bytes 327680 | tf_op jit(solution)/shard_map/while/body/eval_jaxpr/all_gather | solution.py:63
  169.6 0.8 broadcast_multiply_fusion.5
  170.6 1.4 fusion.111
  172.1 5.9 %all_gather.33 = bf16[1,64,2048]{2,1,0:T(8,128)(2,1)S(1)} all-gather(bf16[1,64,512]{2,1,0:T(8,128)(2,1)S(1)} %fusion.112), channel_id=1, replica_groups=mesh['sub'=8,'blk'=4] {'blk'}, dimensions={2}, use_global_device_ids=true | all-gather | bytes 327680 | tf_op jit(solution)/shard_map/while/body/eval_jaxpr/all_gather | solution.py:63
  178.9 0.8 broadcast_multiply_fusion.5
  179.8 1.4 fusion.111
  181.3 5.9 %all_gather.33 = bf16[1,64,2048]{2,1,0:T(8,128)(2,1)S(1)} all-gather(bf16[1,64,512]{2,1,0:T(8,128)(2,1)S(1)} %fusion.112), channel_id=1, replica_groups=mesh['sub'=8,'blk'=4] {'blk'}, dimensions={2}, use_global_device_ids=true | all-gather | bytes 327680 | tf_op jit(solution)/shard_map/while/body/eval_jaxpr/all_gather | solution.py:63
  188.1 0.8 broadcast_multiply_fusion.5
  189.1 1.4 fusion.111
  190.6 5.9 %all_gather.33 = bf16[1,64,2048]{2,1,0:T(8,128)(2,1)S(1)} all-gather(bf16[1,64,512]{2,1,0:T(8,128)(2,1)S(1)} %fusion.112), channel_id=1, replica_groups=mesh['sub'=8,'blk'=4] {'blk'}, dimensions={2}, use_global_device_ids=true | all-gather | bytes 327680 | tf_op jit(solution)/shard_map/while/body/eval_jaxpr/all_gather | solution.py:63
  197.3 0.8 broadcast_multiply_fusion.5
  198.3 1.4 fusion.111
  199.8 5.9 %all_gather.33 = bf16[1,64,2048]{2,1,0:T(8,128)(2,1)S(1)} all-gather(bf16[1,64,512]{2,1,0:T(8,128)(2,1)S(1)} %fusion.112), channel_id=1, replica_groups=mesh['sub'=8,'blk'=4] {'blk'}, dimensions={2}, use_global_device_ids=true | all-gather | bytes 327680 | tf_op jit(solution)/shard_map/while/body/eval_jaxpr/all_gather | solution.py:63
  206.6 0.8 broadcast_multiply_fusion.5
  207.5 1.4 fusion.111
  209.0 5.9 %all_gather.33 = bf16[1,64,2048]{2,1,0:T(8,128)(2,1)S(1)} all-gather(bf16[1,64,512]{2,1,0:T(8,128)(2,1)S(1)} %fusion.112), channel_id=1, replica_groups=mesh['sub'=8,'blk'=4] {'blk'}, dimensions={2}, use_global_device_ids=true | all-gather | bytes 327680 | tf_op jit(solution)/shard_map/while/body/eval_jaxpr/all_gather | solution.py:63
  (215 shorter events, 23.2 us)
Async XLA Ops:
  36.2 8.5 %copy-start = (bf16[1,2048,512]{2,1,0:T(8,128)(2,1)S(1)}, bf16[1,2048,512]{2,1,0:T(8,128)(2,1)}, u32[]{:S(2)}) copy-start(bf16[1,2048,512]{2,1,0:T(8,128)(2,1)} %get-tuple-element.845) | copy-start | bytes 6291460 | tf_op jit(solution)/shard_map/while
  36.2 8.5 %copy-start.3 = (f32[1,512]{1,0:T(1,128)S(1)}, f32[1,512]{1,0:T(1,128)}, u32[]{:S(2)}) copy-start(f32[1,512]{1,0:T(1,128)} %get-tuple-element.839) | copy-start | bytes 6148 | tf_op jit(solution)/shard_map/while
  45.4 8.6 %copy-start = (bf16[1,2048,512]{2,1,0:T(8,128)(2,1)S(1)}, bf16[1,2048,512]{2,1,0:T(8,128)(2,1)}, u32[]{:S(2)}) copy-start(bf16[1,2048,512]{2,1,0:T(8,128)(2,1)} %get-tuple-element.845) | copy-start | bytes 6291460 | tf_op jit(solution)/shard_map/while
  45.4 8.6 %copy-start.3 = (f32[1,512]{1,0:T(1,128)S(1)}, f32[1,512]{1,0:T(1,128)}, u32[]{:S(2)}) copy-start(f32[1,512]{1,0:T(1,128)} %get-tuple-element.839) | copy-start | bytes 6148 | tf_op jit(solution)/shard_map/while
  54.6 8.6 %copy-start = (bf16[1,2048,512]{2,1,0:T(8,128)(2,1)S(1)}, bf16[1,2048,512]{2,1,0:T(8,128)(2,1)}, u32[]{:S(2)}) copy-start(bf16[1,2048,512]{2,1,0:T(8,128)(2,1)} %get-tuple-element.845) | copy-start | bytes 6291460 | tf_op jit(solution)/shard_map/while
  54.6 8.5 %copy-start.3 = (f32[1,512]{1,0:T(1,128)S(1)}, f32[1,512]{1,0:T(1,128)}, u32[]{:S(2)}) copy-start(f32[1,512]{1,0:T(1,128)} %get-tuple-element.839) | copy-start | bytes 6148 | tf_op jit(solution)/shard_map/while
  63.9 8.6 %copy-start = (bf16[1,2048,512]{2,1,0:T(8,128)(2,1)S(1)}, bf16[1,2048,512]{2,1,0:T(8,128)(2,1)}, u32[]{:S(2)}) copy-start(bf16[1,2048,512]{2,1,0:T(8,128)(2,1)} %get-tuple-element.845) | copy-start | bytes 6291460 | tf_op jit(solution)/shard_map/while
  63.9 8.6 %copy-start.3 = (f32[1,512]{1,0:T(1,128)S(1)}, f32[1,512]{1,0:T(1,128)}, u32[]{:S(2)}) copy-start(f32[1,512]{1,0:T(1,128)} %get-tuple-element.839) | copy-start | bytes 6148 | tf_op jit(solution)/shard_map/while
  73.1 8.6 %copy-start = (bf16[1,2048,512]{2,1,0:T(8,128)(2,1)S(1)}, bf16[1,2048,512]{2,1,0:T(8,128)(2,1)}, u32[]{:S(2)}) copy-start(bf16[1,2048,512]{2,1,0:T(8,128)(2,1)} %get-tuple-element.845) | copy-start | bytes 6291460 | tf_op jit(solution)/shard_map/while
  73.1 8.6 %copy-start.3 = (f32[1,512]{1,0:T(1,128)S(1)}, f32[1,512]{1,0:T(1,128)}, u32[]{:S(2)}) copy-start(f32[1,512]{1,0:T(1,128)} %get-tuple-element.839) | copy-start | bytes 6148 | tf_op jit(solution)/shard_map/while
  82.3 8.6 %copy-start = (bf16[1,2048,512]{2,1,0:T(8,128)(2,1)S(1)}, bf16[1,2048,512]{2,1,0:T(8,128)(2,1)}, u32[]{:S(2)}) copy-start(bf16[1,2048,512]{2,1,0:T(8,128)(2,1)} %get-tuple-element.845) | copy-start | bytes 6291460 | tf_op jit(solution)/shard_map/while
  82.3 8.5 %copy-start.3 = (f32[1,512]{1,0:T(1,128)S(1)}, f32[1,512]{1,0:T(1,128)}, u32[]{:S(2)}) copy-start(f32[1,512]{1,0:T(1,128)} %get-tuple-element.839) | copy-start | bytes 6148 | tf_op jit(solution)/shard_map/while
  91.6 8.6 %copy-start = (bf16[1,2048,512]{2,1,0:T(8,128)(2,1)S(1)}, bf16[1,2048,512]{2,1,0:T(8,128)(2,1)}, u32[]{:S(2)}) copy-start(bf16[1,2048,512]{2,1,0:T(8,128)(2,1)} %get-tuple-element.845) | copy-start | bytes 6291460 | tf_op jit(solution)/shard_map/while
  91.6 8.5 %copy-start.3 = (f32[1,512]{1,0:T(1,128)S(1)}, f32[1,512]{1,0:T(1,128)}, u32[]{:S(2)}) copy-start(f32[1,512]{1,0:T(1,128)} %get-tuple-element.839) | copy-start | bytes 6148 | tf_op jit(solution)/shard_map/while
  100.8 8.6 %copy-start = (bf16[1,2048,512]{2,1,0:T(8,128)(2,1)S(1)}, bf16[1,2048,512]{2,1,0:T(8,128)(2,1)}, u32[]{:S(2)}) copy-start(bf16[1,2048,512]{2,1,0:T(8,128)(2,1)} %get-tuple-element.845) | copy-start | bytes 6291460 | tf_op jit(solution)/shard_map/while
  100.8 8.5 %copy-start.3 = (f32[1,512]{1,0:T(1,128)S(1)}, f32[1,512]{1,0:T(1,128)}, u32[]{:S(2)}) copy-start(f32[1,512]{1,0:T(1,128)} %get-tuple-element.839) | copy-start | bytes 6148 | tf_op jit(solution)/shard_map/while
  141.8 8.5 %copy-start.1 = (bf16[1,2048,512]{2,1,0:T(8,128)(2,1)S(1)}, bf16[1,2048,512]{2,1,0:T(8,128)(2,1)}, u32[]{:S(2)}) copy-start(bf16[1,2048,512]{2,1,0:T(8,128)(2,1)} %get-tuple-element.887) | copy-start | bytes 6291460 | tf_op jit(solution)/shard_map/while
  141.8 8.5 %copy-start.4 = (f32[1,512]{1,0:T(1,128)S(1)}, f32[1,512]{1,0:T(1,128)}, u32[]{:S(2)}) copy-start(f32[1,512]{1,0:T(1,128)} %get-tuple-element.881) | copy-start | bytes 6148 | tf_op jit(solution)/shard_map/while
  150.9 8.6 %copy-start.1 = (bf16[1,2048,512]{2,1,0:T(8,128)(2,1)S(1)}, bf16[1,2048,512]{2,1,0:T(8,128)(2,1)}, u32[]{:S(2)}) copy-start(bf16[1,2048,512]{2,1,0:T(8,128)(2,1)} %get-tuple-element.887) | copy-start | bytes 6291460 | tf_op jit(solution)/shard_map/while
  150.9 8.6 %copy-start.4 = (f32[1,512]{1,0:T(1,128)S(1)}, f32[1,512]{1,0:T(1,128)}, u32[]{:S(2)}) copy-start(f32[1,512]{1,0:T(1,128)} %get-tuple-element.881) | copy-start | bytes 6148 | tf_op jit(solution)/shard_map/while
  160.1 8.6 %copy-start.1 = (bf16[1,2048,512]{2,1,0:T(8,128)(2,1)S(1)}, bf16[1,2048,512]{2,1,0:T(8,128)(2,1)}, u32[]{:S(2)}) copy-start(bf16[1,2048,512]{2,1,0:T(8,128)(2,1)} %get-tuple-element.887) | copy-start | bytes 6291460 | tf_op jit(solution)/shard_map/while
  160.2 8.6 %copy-start.4 = (f32[1,512]{1,0:T(1,128)S(1)}, f32[1,512]{1,0:T(1,128)}, u32[]{:S(2)}) copy-start(f32[1,512]{1,0:T(1,128)} %get-tuple-element.881) | copy-start | bytes 6148 | tf_op jit(solution)/shard_map/while
  169.4 8.6 %copy-start.1 = (bf16[1,2048,512]{2,1,0:T(8,128)(2,1)S(1)}, bf16[1,2048,512]{2,1,0:T(8,128)(2,1)}, u32[]{:S(2)}) copy-start(bf16[1,2048,512]{2,1,0:T(8,128)(2,1)} %get-tuple-element.887) | copy-start | bytes 6291460 | tf_op jit(solution)/shard_map/while
  169.4 8.6 %copy-start.4 = (f32[1,512]{1,0:T(1,128)S(1)}, f32[1,512]{1,0:T(1,128)}, u32[]{:S(2)}) copy-start(f32[1,512]{1,0:T(1,128)} %get-tuple-element.881) | copy-start | bytes 6148 | tf_op jit(solution)/shard_map/while
  178.6 8.6 %copy-start.1 = (bf16[1,2048,512]{2,1,0:T(8,128)(2,1)S(1)}, bf16[1,2048,512]{2,1,0:T(8,128)(2,1)}, u32[]{:S(2)}) copy-start(bf16[1,2048,512]{2,1,0:T(8,128)(2,1)} %get-tuple-element.887) | copy-start | bytes 6291460 | tf_op jit(solution)/shard_map/while
  178.6 8.6 %copy-start.4 = (f32[1,512]{1,0:T(1,128)S(1)}, f32[1,512]{1,0:T(1,128)}, u32[]{:S(2)}) copy-start(f32[1,512]{1,0:T(1,128)} %get-tuple-element.881) | copy-start | bytes 6148 | tf_op jit(solution)/shard_map/while
  187.9 8.6 %copy-start.1 = (bf16[1,2048,512]{2,1,0:T(8,128)(2,1)S(1)}, bf16[1,2048,512]{2,1,0:T(8,128)(2,1)}, u32[]{:S(2)}) copy-start(bf16[1,2048,512]{2,1,0:T(8,128)(2,1)} %get-tuple-element.887) | copy-start | bytes 6291460 | tf_op jit(solution)/shard_map/while
  187.9 8.6 %copy-start.4 = (f32[1,512]{1,0:T(1,128)S(1)}, f32[1,512]{1,0:T(1,128)}, u32[]{:S(2)}) copy-start(f32[1,512]{1,0:T(1,128)} %get-tuple-element.881) | copy-start | bytes 6148 | tf_op jit(solution)/shard_map/while
  197.1 8.6 %copy-start.1 = (bf16[1,2048,512]{2,1,0:T(8,128)(2,1)S(1)}, bf16[1,2048,512]{2,1,0:T(8,128)(2,1)}, u32[]{:S(2)}) copy-start(bf16[1,2048,512]{2,1,0:T(8,128)(2,1)} %get-tuple-element.887) | copy-start | bytes 6291460 | tf_op jit(solution)/shard_map/while
  197.1 8.6 %copy-start.4 = (f32[1,512]{1,0:T(1,128)S(1)}, f32[1,512]{1,0:T(1,128)}, u32[]{:S(2)}) copy-start(f32[1,512]{1,0:T(1,128)} %get-tuple-element.881) | copy-start | bytes 6148 | tf_op jit(solution)/shard_map/while
  206.3 8.6 %copy-start.1 = (bf16[1,2048,512]{2,1,0:T(8,128)(2,1)S(1)}, bf16[1,2048,512]{2,1,0:T(8,128)(2,1)}, u32[]{:S(2)}) copy-start(bf16[1,2048,512]{2,1,0:T(8,128)(2,1)} %get-tuple-element.887) | copy-start | bytes 6291460 | tf_op jit(solution)/shard_map/while
  206.3 8.6 %copy-start.4 = (f32[1,512]{1,0:T(1,128)S(1)}, f32[1,512]{1,0:T(1,128)}, u32[]{:S(2)}) copy-start(f32[1,512]{1,0:T(1,128)} %get-tuple-element.881) | copy-start | bytes 6148 | tf_op jit(solution)/shard_map/while
  215.6 1.0 copy-start.2
where the time goes:
time: 217 us
  blocking collectives  157 us (72%)
  matrix products  35 us (16%)
  other arithmetic  15 us (7%)
  local copies, waits for them, and re-layouts  6.51 us (3%)
    all_gather x16, blocking collectives, advance(): lax.all_gather(loop_argument, 'blk', axis=2, tiled=True)  93.5 us
    all_gather x2, blocking collectives, port_fetch(): lax.all_gather(waves, 'sub', axis=0, tiled=True)  63.5 us
    dot_general x16, matrix products, advance(): jnp.einsum('qf,qfcn->qcn', chosen.astype(jnp.bfloat16), source, preferred...  23.2 us
    mul x16, other arithmetic, advance(): coupling[:, :, None]  13.5 us
    dot_general x16, matrix products, contract(): jnp.einsum('qcn,qnm->qcm', shard_rows, inverse_off, preferred_element_typ...  7.7 us

commit v1 on v0

--- a/solution.py
+++ b/solution.py
@@ -4,6 +4,22 @@
 from jax.sharding import PartitionSpec as P
 
 SWEEPS = 2
+
+
+def summed_both_ways(array, axis, dim, term):
+    size, index, rows = (lax.axis_size(axis), lax.axis_index(axis), array.shape[dim])
+    right = [(i, (i + 1) % size) for i in range(size)]
+    left = [(i, (i - 1) % size) for i in range(size)]
+    middle = size // 2
+    from_left = from_right = array
+    total = term(array, index * rows)
+    for step in range(1, middle + 1):
+        from_left = lax.ppermute(from_left, axis, right)
+        if step < size - middle:
+            from_right = lax.ppermute(from_right, axis, left)
+            total = total + term(from_right, (index + step) % size * rows)
+        total = total + term(from_left, (index - step) % size * rows)
+    return total
 
 
 def step_count(bucket, refined_points):
@@ -15,11 +31,16 @@
 
 
 def port_fetch(waves, selector):
-    return jnp.einsum(
-        "qjr,rjc->qjc",
-        selector,
-        lax.all_gather(waves, "sub", axis=0, tiled=True),
-        preferred_element_type=jnp.float32,
+    return summed_both_ways(
+        waves,
+        "sub",
+        0,
+        lambda shard, start: jnp.einsum(
+            "qjr,rjc->qjc",
+            lax.dynamic_slice_in_dim(selector, start, shard.shape[0], axis=2),
+            shard,
+            preferred_element_type=jnp.float32,
+        ),
     ).astype(jnp.bfloat16)
 
 

time: 217 us -> 207 us (0.954)
  blocking collectives: 157 us -> 93.6 us
  starting transfers between devices: 0 us -> 29.7 us
  waiting for transfers between devices: 0 us -> 22.9 us
    all_gather x2 -> x0, blocking collectives: 63.5 us -> none  [port_fetch(): lax.all_gather(waves, 'sub', axis=0, tiled=True)]
    ppermute x0 -> x14, starting transfers between devices: none -> 29.7 us  [the longest x6 26.6 us: summed_both_ways(): from_right = lax.ppermute(from_right, axis, left)]
    ppermute x0 -> x14, waiting for transfers between devices: none -> 22.9 us  [the longest x8 22.6 us: summed_both_ways(): from_left = lax.ppermute(from_left, axis, right)]
  transfers between devices with their start and end apart: 0 -> 14, of which waited for: 0 -> 9; matrix products, arithmetic and copies ran while one was open for 0% -> 0% of each run, Pallas kernels for 0% -> 0%
where the time goes in v1:
time: 207 us; the launch traced here: 206 us
  blocking collectives  93.6 us (45%)
  matrix products  34.5 us (17%)
  starting transfers between devices  29.7 us (14%)
  waiting for transfers between devices  22.9 us (11%)
  other arithmetic  15.9 us (8%)
  local copies, waits for them, and re-layouts  6.61 us (3%)
    all_gather x16, blocking collectives, advance(): lax.all_gather(loop_argument, 'blk', axis=2, tiled=True)  93.6 us
    ppermute x6, starting transfers between devices, summed_both_ways(): from_right = lax.ppermute(from_right, axis, left)  26.6 us
    dot_general x16, matrix products, advance(): jnp.einsum('qf,qfcn->qcn', chosen.astype(jnp.bfloat16), source, preferred...  23.2 us
    ppermute x8, waiting for transfers between devices, summed_both_ways(): from_left = lax.ppermute(from_left, axis, right)  22.6 us
    mul x16, other arithmetic, advance(): coupling[:, :, None]  13.5 us
    dot_general x16, matrix products, contract(): jnp.einsum('qcn,qnm->qcm', shard_rows, inverse_off, preferred_element_typ...  7.7 us
  transfers between devices with their start and end apart: 14, of which 9 were waited for; matrix products, arithmetic and copies ran while one was open for 0% of the time, Pallas kernels for 0%

profile of v1, /device:TPU:0, one launch (start us, length us, event | category | flops | bytes accessed | tf_op | source)
XLA Modules:
  0.0 206.4 jit_solution(12971529277287693106)
XLA Ops:
  1.5 3.0 %collective-permute-start.1 = (bf16[1,32,512]{2,1,0:T(8,128)(2,1)}, bf16[1,32,512]{2,1,0:T(8,128)(2,1)S(1)}, u32[]{:S(2)}, u32[]{:S(2)}) collective-permute-start(bf16[1,32,512]{2,1,0:T(8,128)(2,1)} %param.20), channel_id=1, source_target_pairs={{0,4},{4,8},{8,12},{12,16},{16,20},{20,24},{24,28},{28,0},{1,5},{5... | collective-permute-start | bytes 98312 | tf_op jit(solution)/shard_map/ppermute | solution.py:17
  4.5 3.0 %collective-permute-start = (bf16[1,32,512]{2,1,0:T(8,128)(2,1)}, bf16[1,32,512]{2,1,0:T(8,128)(2,1)S(1)}, u32[]{:S(2)}, u32[]{:S(2)}) collective-permute-start(bf16[1,32,512]{2,1,0:T(8,128)(2,1)} %param.20), channel_id=1, source_target_pairs={{0,28},{4,0},{8,4},{12,8},{16,12},{20,16},{24,20},{28,24},{1,29},{... | collective-permute-start | bytes 98312 | tf_op jit(solution)/shard_map/ppermute | solution.py:19
  8.3 1.3 collective-permute-done.1
  9.8 4.6 %collective-permute-start.2 = (bf16[1,32,512]{2,1,0:T(8,128)(2,1)S(1)}, bf16[1,32,512]{2,1,0:T(8,128)(2,1)S(1)}, u32[]{:S(2)}, u32[]{:S(2)}) collective-permute-start(bf16[1,32,512]{2,1,0:T(8,128)(2,1)S(1)} %collective-permute-done), channel_id=1, source_target_pairs={{0,28},{4,0},{8,4},{12,8},{16,12},{20,16},{24,20},{28,24},{1,29},{... | collective-permute-start | bytes 98312 | tf_op jit(solution)/shard_map/ppermute | solution.py:19
  14.5 1.8 collective-permute-done.3
  17.0 4.8 %collective-permute-start.4 = (bf16[1,32,512]{2,1,0:T(8,128)(2,1)S(1)}, bf16[1,32,512]{2,1,0:T(8,128)(2,1)S(1)}, u32[]{:S(2)}, u32[]{:S(2)}) collective-permute-start(bf16[1,32,512]{2,1,0:T(8,128)(2,1)S(1)} %collective-permute-done.2), channel_id=1, source_target_pairs={{0,28},{4,0},{8,4},{12,8},{16,12},{20,16},{24,20},{28,24},{1,29},{... | collective-permute-start | bytes 98312 | tf_op jit(solution)/shard_map/ppermute | solution.py:19
  23.4 6.1 %collective-permute-done.6 = bf16[1,32,512]{2,1,0:T(8,128)(2,1)S(1)} collective-permute-done((bf16[1,32,512]{2,1,0:T(8,128)(2,1)S(1)}, bf16[1,32,512]{2,1,0:T(8,128)(2,1)S(1)}, u32[]{:S(2)}, u32[]{:S(2)}) %collective-permute-start.6) | collective-permute-done | bytes 32800 | tf_op jit(solution)/shard_map/ppermute | solution.py:17
  30.5 73.9 %while.36 = (s32[]{:T(128)}, f32[1,64,512]{2,1,0:T(8,128)S(1)}, f32[1,8,64,32]{2,3,1,0:T(8,128)S(1)}, s32[1]{0:T(128)}, f32[1,512]{1,0:T(1,128)}, /*index=5*/f32...) while((s32[]{:T(128)}, f32[1,64,512]{2,1,0:T(8,128)S(1)}, ...), condition=%wide.region_2.3_spmd.clone, body=%wide.region_1.2_spmd.clone.sunk | while | flops 135202832 | bytes 13330811 | solution.py:94
  31.7 1.4 fusion.126
  33.2 5.9 %all_gather.24 = bf16[1,64,2048]{2,1,0:T(8,128)(2,1)S(1)} all-gather(bf16[1,64,512]{2,1,0:T(8,128)(2,1)S(1)} %fusion.127), channel_id=1, replica_groups=mesh['sub'=8,'blk'=4] {'blk'}, dimensions={2}, use_global_device_ids=true | all-gather | bytes 327680 | tf_op jit(solution)/shard_map/while/body/eval_jaxpr/all_gather | solution.py:84
  41.0 1.4 fusion.126
  42.5 5.9 %all_gather.24 = bf16[1,64,2048]{2,1,0:T(8,128)(2,1)S(1)} all-gather(bf16[1,64,512]{2,1,0:T(8,128)(2,1)S(1)} %fusion.127), channel_id=1, replica_groups=mesh['sub'=8,'blk'=4] {'blk'}, dimensions={2}, use_global_device_ids=true | all-gather | bytes 327680 | tf_op jit(solution)/shard_map/while/body/eval_jaxpr/all_gather | solution.py:84
  50.3 1.4 fusion.126
  51.7 5.9 %all_gather.24 = bf16[1,64,2048]{2,1,0:T(8,128)(2,1)S(1)} all-gather(bf16[1,64,512]{2,1,0:T(8,128)(2,1)S(1)} %fusion.127), channel_id=1, replica_groups=mesh['sub'=8,'blk'=4] {'blk'}, dimensions={2}, use_global_device_ids=true | all-gather | bytes 327680 | tf_op jit(solution)/shard_map/while/body/eval_jaxpr/all_gather | solution.py:84
  59.5 1.4 fusion.126
  61.0 5.9 %all_gather.24 = bf16[1,64,2048]{2,1,0:T(8,128)(2,1)S(1)} all-gather(bf16[1,64,512]{2,1,0:T(8,128)(2,1)S(1)} %fusion.127), channel_id=1, replica_groups=mesh['sub'=8,'blk'=4] {'blk'}, dimensions={2}, use_global_device_ids=true | all-gather | bytes 327680 | tf_op jit(solution)/shard_map/while/body/eval_jaxpr/all_gather | solution.py:84
  68.7 1.4 fusion.126
  70.2 5.9 %all_gather.24 = bf16[1,64,2048]{2,1,0:T(8,128)(2,1)S(1)} all-gather(bf16[1,64,512]{2,1,0:T(8,128)(2,1)S(1)} %fusion.127), channel_id=1, replica_groups=mesh['sub'=8,'blk'=4] {'blk'}, dimensions={2}, use_global_device_ids=true | all-gather | bytes 327680 | tf_op jit(solution)/shard_map/while/body/eval_jaxpr/all_gather | solution.py:84
  78.0 1.4 fusion.126
  79.4 5.9 %all_gather.24 = bf16[1,64,2048]{2,1,0:T(8,128)(2,1)S(1)} all-gather(bf16[1,64,512]{2,1,0:T(8,128)(2,1)S(1)} %fusion.127), channel_id=1, replica_groups=mesh['sub'=8,'blk'=4] {'blk'}, dimensions={2}, use_global_device_ids=true | all-gather | bytes 327680 | tf_op jit(solution)/shard_map/while/body/eval_jaxpr/all_gather | solution.py:84
  87.2 1.4 fusion.126
  88.7 5.9 %all_gather.24 = bf16[1,64,2048]{2,1,0:T(8,128)(2,1)S(1)} all-gather(bf16[1,64,512]{2,1,0:T(8,128)(2,1)S(1)} %fusion.127), channel_id=1, replica_groups=mesh['sub'=8,'blk'=4] {'blk'}, dimensions={2}, use_global_device_ids=true | all-gather | bytes 327680 | tf_op jit(solution)/shard_map/while/body/eval_jaxpr/all_gather | solution.py:84
  96.4 1.4 fusion.126
  97.9 5.9 %all_gather.24 = bf16[1,64,2048]{2,1,0:T(8,128)(2,1)S(1)} all-gather(bf16[1,64,512]{2,1,0:T(8,128)(2,1)S(1)} %fusion.127), channel_id=1, replica_groups=mesh['sub'=8,'blk'=4] {'blk'}, dimensions={2}, use_global_device_ids=true | all-gather | bytes 327680 | tf_op jit(solution)/shard_map/while/body/eval_jaxpr/all_gather | solution.py:84
  104.9 4.7 %collective-permute-start.7 = (bf16[1,32,512]{2,1,0:T(8,128)(2,1)S(1)}, bf16[1,32,512]{2,1,0:T(8,128)(2,1)S(1)}, u32[]{:S(2)}, u32[]{:S(2)}) collective-permute-start(bf16[1,32,512]{2,1,0:T(8,128)(2,1)S(1)} %convert_element_type.109), channel_id=1, source_target_pairs={{0,28},{4,0},{8,4},{12,8},{16,12},{20,16},{24,20},{28,24},{1,29},{... | collective-permute-start | bytes 98312 | tf_op jit(solution)/shard_map/ppermute | solution.py:19
  109.6 1.9 collective-permute-done.8
  111.5 4.7 %collective-permute-start.9 = (bf16[1,32,512]{2,1,0:T(8,128)(2,1)S(1)}, bf16[1,32,512]{2,1,0:T(8,128)(2,1)S(1)}, u32[]{:S(2)}, u32[]{:S(2)}) collective-permute-start(bf16[1,32,512]{2,1,0:T(8,128)(2,1)S(1)} %collective-permute-done.7), channel_id=1, source_target_pairs={{0,28},{4,0},{8,4},{12,8},{16,12},{20,16},{24,20},{28,24},{1,29},{... | collective-permute-start | bytes 98312 | tf_op jit(solution)/shard_map/ppermute | solution.py:19
  116.2 1.9 collective-permute-done.10
  118.1 4.7 %collective-permute-start.11 = (bf16[1,32,512]{2,1,0:T(8,128)(2,1)S(1)}, bf16[1,32,512]{2,1,0:T(8,128)(2,1)S(1)}, u32[]{:S(2)}, u32[]{:S(2)}) collective-permute-start(bf16[1,32,512]{2,1,0:T(8,128)(2,1)S(1)} %collective-permute-done.9), channel_id=1, source_target_pairs={{0,28},{4,0},{8,4},{12,8},{16,12},{20,16},{24,20},{28,24},{1,29},{... | collective-permute-start | bytes 98312 | tf_op jit(solution)/shard_map/ppermute | solution.py:19
  122.8 1.9 collective-permute-done.12
  124.8 6.5 %collective-permute-done.13 = bf16[1,32,512]{2,1,0:T(8,128)(2,1)S(1)} collective-permute-done((bf16[1,32,512]{2,1,0:T(8,128)(2,1)S(1)}, bf16[1,32,512]{2,1,0:T(8,128)(2,1)S(1)}, u32[]{:S(2)}, u32[]{:S(2)}) %collective-permute-start.13) | collective-permute-done | bytes 32800 | tf_op jit(solution)/shard_map/ppermute | solution.py:17
  131.6 73.8 %while.37 = (s32[]{:T(128)}, f32[1,64,512]{2,1,0:T(8,128)S(1)}, f32[1,8,64,32]{2,3,1,0:T(8,128)S(1)}, s32[1]{0:T(128)}, f32[1,512]{1,0:T(1,128)}, /*index=5*/f32...) while((s32[]{:T(128)}, f32[1,64,512]{2,1,0:T(8,128)S(1)}, ...), condition=%wide.region_4.6_spmd.clone, body=%wide.region_3.5_spmd.clone.sunk | while | flops 135202832 | bytes 13330811 | solution.py:94
  132.8 1.4 fusion.136
  134.3 5.8 %all_gather.25 = bf16[1,64,2048]{2,1,0:T(8,128)(2,1)S(1)} all-gather(bf16[1,64,512]{2,1,0:T(8,128)(2,1)S(1)} %fusion.137), channel_id=1, replica_groups=mesh['sub'=8,'blk'=4] {'blk'}, dimensions={2}, use_global_device_ids=true | all-gather | bytes 327680 | tf_op jit(solution)/shard_map/while/body/eval_jaxpr/all_gather | solution.py:84
  142.0 1.4 fusion.136
  143.4 5.9 %all_gather.25 = bf16[1,64,2048]{2,1,0:T(8,128)(2,1)S(1)} all-gather(bf16[1,64,512]{2,1,0:T(8,128)(2,1)S(1)} %fusion.137), channel_id=1, replica_groups=mesh['sub'=8,'blk'=4] {'blk'}, dimensions={2}, use_global_device_ids=true | all-gather | bytes 327680 | tf_op jit(solution)/shard_map/while/body/eval_jaxpr/all_gather | solution.py:84
  151.2 1.4 fusion.136
  152.7 5.9 %all_gather.25 = bf16[1,64,2048]{2,1,0:T(8,128)(2,1)S(1)} all-gather(bf16[1,64,512]{2,1,0:T(8,128)(2,1)S(1)} %fusion.137), channel_id=1, replica_groups=mesh['sub'=8,'blk'=4] {'blk'}, dimensions={2}, use_global_device_ids=true | all-gather | bytes 327680 | tf_op jit(solution)/shard_map/while/body/eval_jaxpr/all_gather | solution.py:84
  160.4 1.4 fusion.136
  161.9 5.9 %all_gather.25 = bf16[1,64,2048]{2,1,0:T(8,128)(2,1)S(1)} all-gather(bf16[1,64,512]{2,1,0:T(8,128)(2,1)S(1)} %fusion.137), channel_id=1, replica_groups=mesh['sub'=8,'blk'=4] {'blk'}, dimensions={2}, use_global_device_ids=true | all-gather | bytes 327680 | tf_op jit(solution)/shard_map/while/body/eval_jaxpr/all_gather | solution.py:84
  169.7 1.4 fusion.136
  171.2 5.9 %all_gather.25 = bf16[1,64,2048]{2,1,0:T(8,128)(2,1)S(1)} all-gather(bf16[1,64,512]{2,1,0:T(8,128)(2,1)S(1)} %fusion.137), channel_id=1, replica_groups=mesh['sub'=8,'blk'=4] {'blk'}, dimensions={2}, use_global_device_ids=true | all-gather | bytes 327680 | tf_op jit(solution)/shard_map/while/body/eval_jaxpr/all_gather | solution.py:84
  178.9 1.4 fusion.136
  180.4 5.9 %all_gather.25 = bf16[1,64,2048]{2,1,0:T(8,128)(2,1)S(1)} all-gather(bf16[1,64,512]{2,1,0:T(8,128)(2,1)S(1)} %fusion.137), channel_id=1, replica_groups=mesh['sub'=8,'blk'=4] {'blk'}, dimensions={2}, use_global_device_ids=true | all-gather | bytes 327680 | tf_op jit(solution)/shard_map/while/body/eval_jaxpr/all_gather | solution.py:84
  188.1 1.4 fusion.136
  189.6 5.9 %all_gather.25 = bf16[1,64,2048]{2,1,0:T(8,128)(2,1)S(1)} all-gather(bf16[1,64,512]{2,1,0:T(8,128)(2,1)S(1)} %fusion.137), channel_id=1, replica_groups=mesh['sub'=8,'blk'=4] {'blk'}, dimensions={2}, use_global_device_ids=true | all-gather | bytes 327680 | tf_op jit(solution)/shard_map/while/body/eval_jaxpr/all_gather | solution.py:84
  197.4 1.4 fusion.136
  198.9 5.9 %all_gather.25 = bf16[1,64,2048]{2,1,0:T(8,128)(2,1)S(1)} all-gather(bf16[1,64,512]{2,1,0:T(8,128)(2,1)S(1)} %fusion.137), channel_id=1, replica_groups=mesh['sub'=8,'blk'=4] {'blk'}, dimensions={2}, use_global_device_ids=true | all-gather | bytes 327680 | tf_op jit(solution)/shard_map/while/body/eval_jaxpr/all_gather | solution.py:84
  (241 shorter events, 35.4 us)
Async XLA Ops:
  1.5 8.1 %collective-permute-start.1 = (bf16[1,32,512]{2,1,0:T(8,128)(2,1)}, bf16[1,32,512]{2,1,0:T(8,128)(2,1)S(1)}, u32[]{:S(2)}, u32[]{:S(2)}) collective-permute-start(bf16[1,32,512]{2,1,0:T(8,128)(2,1)} %param.20), channel_id=1, source_target_pairs={{0,4},{4,8},{8,12},{12,16},{16,20},{20,24},{24,28},{28,0},{1,5},{5... | collective-permute-start | bytes 98312 | tf_op jit(solution)/shard_map/ppermute | solution.py:17
  4.5 5.3 %collective-permute-start = (bf16[1,32,512]{2,1,0:T(8,128)(2,1)}, bf16[1,32,512]{2,1,0:T(8,128)(2,1)S(1)}, u32[]{:S(2)}, u32[]{:S(2)}) collective-permute-start(bf16[1,32,512]{2,1,0:T(8,128)(2,1)} %param.20), channel_id=1, source_target_pairs={{0,28},{4,0},{8,4},{12,8},{16,12},{20,16},{24,20},{28,24},{1,29},{... | collective-permute-start | bytes 98312 | tf_op jit(solution)/shard_map/ppermute | solution.py:19
  9.7 6.6 %collective-permute-start.3 = (bf16[1,32,512]{2,1,0:T(8,128)(2,1)S(1)}, bf16[1,32,512]{2,1,0:T(8,128)(2,1)S(1)}, u32[]{:S(2)}, u32[]{:S(2)}) collective-permute-start(bf16[1,32,512]{2,1,0:T(8,128)(2,1)S(1)} %collective-permute-done.1), channel_id=1, source_target_pairs={{0,4},{4,8},{8,12},{12,16},{16,20},{20,24},{24,28},{28,0},{1,5},{5... | collective-permute-start | bytes 98312 | tf_op jit(solution)/shard_map/ppermute | solution.py:17
  9.8 7.2 %collective-permute-start.2 = (bf16[1,32,512]{2,1,0:T(8,128)(2,1)S(1)}, bf16[1,32,512]{2,1,0:T(8,128)(2,1)S(1)}, u32[]{:S(2)}, u32[]{:S(2)}) collective-permute-start(bf16[1,32,512]{2,1,0:T(8,128)(2,1)S(1)} %collective-permute-done), channel_id=1, source_target_pairs={{0,28},{4,0},{8,4},{12,8},{16,12},{20,16},{24,20},{28,24},{1,29},{... | collective-permute-start | bytes 98312 | tf_op jit(solution)/shard_map/ppermute | solution.py:19
  16.3 6.6 %collective-permute-start.5 = (bf16[1,32,512]{2,1,0:T(8,128)(2,1)S(1)}, bf16[1,32,512]{2,1,0:T(8,128)(2,1)S(1)}, u32[]{:S(2)}, u32[]{:S(2)}) collective-permute-start(bf16[1,32,512]{2,1,0:T(8,128)(2,1)S(1)} %collective-permute-done.3), channel_id=1, source_target_pairs={{0,4},{4,8},{8,12},{12,16},{16,20},{20,24},{24,28},{28,0},{1,5},{5... | collective-permute-start | bytes 98312 | tf_op jit(solution)/shard_map/ppermute | solution.py:17
  17.0 6.4 %collective-permute-start.4 = (bf16[1,32,512]{2,1,0:T(8,128)(2,1)S(1)}, bf16[1,32,512]{2,1,0:T(8,128)(2,1)S(1)}, u32[]{:S(2)}, u32[]{:S(2)}) collective-permute-start(bf16[1,32,512]{2,1,0:T(8,128)(2,1)S(1)} %collective-permute-done.2), channel_id=1, source_target_pairs={{0,28},{4,0},{8,4},{12,8},{16,12},{20,16},{24,20},{28,24},{1,29},{... | collective-permute-start | bytes 98312 | tf_op jit(solution)/shard_map/ppermute | solution.py:19
  22.9 6.6 %collective-permute-start.6 = (bf16[1,32,512]{2,1,0:T(8,128)(2,1)S(1)}, bf16[1,32,512]{2,1,0:T(8,128)(2,1)S(1)}, u32[]{:S(2)}, u32[]{:S(2)}) collective-permute-start(bf16[1,32,512]{2,1,0:T(8,128)(2,1)S(1)} %collective-permute-done.5), channel_id=1, source_target_pairs={{0,4},{4,8},{8,12},{12,16},{16,20},{20,24},{24,28},{28,0},{1,5},{5... | collective-permute-start | bytes 98312 | tf_op jit(solution)/shard_map/ppermute | solution.py:17
  30.5 8.6 %copy-start = (bf16[1,2048,512]{2,1,0:T(8,128)(2,1)S(1)}, bf16[1,2048,512]{2,1,0:T(8,128)(2,1)}, u32[]{:S(2)}) copy-start(bf16[1,2048,512]{2,1,0:T(8,128)(2,1)} %get-tuple-element.853) | copy-start | bytes 6291460 | tf_op jit(solution)/shard_map/while
  30.5 8.6 %copy-start.3 = (f32[1,512]{1,0:T(1,128)S(1)}, f32[1,512]{1,0:T(1,128)}, u32[]{:S(2)}) copy-start(f32[1,512]{1,0:T(1,128)} %get-tuple-element.847) | copy-start | bytes 6148 | tf_op jit(solution)/shard_map/while
  39.8 8.6 %copy-start = (bf16[1,2048,512]{2,1,0:T(8,128)(2,1)S(1)}, bf16[1,2048,512]{2,1,0:T(8,128)(2,1)}, u32[]{:S(2)}) copy-start(bf16[1,2048,512]{2,1,0:T(8,128)(2,1)} %get-tuple-element.853) | copy-start | bytes 6291460 | tf_op jit(solution)/shard_map/while
  39.8 8.6 %copy-start.3 = (f32[1,512]{1,0:T(1,128)S(1)}, f32[1,512]{1,0:T(1,128)}, u32[]{:S(2)}) copy-start(f32[1,512]{1,0:T(1,128)} %get-tuple-element.847) | copy-start | bytes 6148 | tf_op jit(solution)/shard_map/while
  49.0 8.6 %copy-start = (bf16[1,2048,512]{2,1,0:T(8,128)(2,1)S(1)}, bf16[1,2048,512]{2,1,0:T(8,128)(2,1)}, u32[]{:S(2)}) copy-start(bf16[1,2048,512]{2,1,0:T(8,128)(2,1)} %get-tuple-element.853) | copy-start | bytes 6291460 | tf_op jit(solution)/shard_map/while
  49.0 8.6 %copy-start.3 = (f32[1,512]{1,0:T(1,128)S(1)}, f32[1,512]{1,0:T(1,128)}, u32[]{:S(2)}) copy-start(f32[1,512]{1,0:T(1,128)} %get-tuple-element.847) | copy-start | bytes 6148 | tf_op jit(solution)/shard_map/while
  58.3 8.6 %copy-start = (bf16[1,2048,512]{2,1,0:T(8,128)(2,1)S(1)}, bf16[1,2048,512]{2,1,0:T(8,128)(2,1)}, u32[]{:S(2)}) copy-start(bf16[1,2048,512]{2,1,0:T(8,128)(2,1)} %get-tuple-element.853) | copy-start | bytes 6291460 | tf_op jit(solution)/shard_map/while
  58.3 8.6 %copy-start.3 = (f32[1,512]{1,0:T(1,128)S(1)}, f32[1,512]{1,0:T(1,128)}, u32[]{:S(2)}) copy-start(f32[1,512]{1,0:T(1,128)} %get-tuple-element.847) | copy-start | bytes 6148 | tf_op jit(solution)/shard_map/while
  67.5 8.6 %copy-start = (bf16[1,2048,512]{2,1,0:T(8,128)(2,1)S(1)}, bf16[1,2048,512]{2,1,0:T(8,128)(2,1)}, u32[]{:S(2)}) copy-start(bf16[1,2048,512]{2,1,0:T(8,128)(2,1)} %get-tuple-element.853) | copy-start | bytes 6291460 | tf_op jit(solution)/shard_map/while
  67.5 8.6 %copy-start.3 = (f32[1,512]{1,0:T(1,128)S(1)}, f32[1,512]{1,0:T(1,128)}, u32[]{:S(2)}) copy-start(f32[1,512]{1,0:T(1,128)} %get-tuple-element.847) | copy-start | bytes 6148 | tf_op jit(solution)/shard_map/while
  76.7 8.6 %copy-start = (bf16[1,2048,512]{2,1,0:T(8,128)(2,1)S(1)}, bf16[1,2048,512]{2,1,0:T(8,128)(2,1)}, u32[]{:S(2)}) copy-start(bf16[1,2048,512]{2,1,0:T(8,128)(2,1)} %get-tuple-element.853) | copy-start | bytes 6291460 | tf_op jit(solution)/shard_map/while
  76.8 8.6 %copy-start.3 = (f32[1,512]{1,0:T(1,128)S(1)}, f32[1,512]{1,0:T(1,128)}, u32[]{:S(2)}) copy-start(f32[1,512]{1,0:T(1,128)} %get-tuple-element.847) | copy-start | bytes 6148 | tf_op jit(solution)/shard_map/while
  86.0 8.6 %copy-start = (bf16[1,2048,512]{2,1,0:T(8,128)(2,1)S(1)}, bf16[1,2048,512]{2,1,0:T(8,128)(2,1)}, u32[]{:S(2)}) copy-start(bf16[1,2048,512]{2,1,0:T(8,128)(2,1)} %get-tuple-element.853) | copy-start | bytes 6291460 | tf_op jit(solution)/shard_map/while
  86.0 8.6 %copy-start.3 = (f32[1,512]{1,0:T(1,128)S(1)}, f32[1,512]{1,0:T(1,128)}, u32[]{:S(2)}) copy-start(f32[1,512]{1,0:T(1,128)} %get-tuple-element.847) | copy-start | bytes 6148 | tf_op jit(solution)/shard_map/while
  95.2 8.6 %copy-start = (bf16[1,2048,512]{2,1,0:T(8,128)(2,1)S(1)}, bf16[1,2048,512]{2,1,0:T(8,128)(2,1)}, u32[]{:S(2)}) copy-start(bf16[1,2048,512]{2,1,0:T(8,128)(2,1)} %get-tuple-element.853) | copy-start | bytes 6291460 | tf_op jit(solution)/shard_map/while
  95.2 8.6 %copy-start.3 = (f32[1,512]{1,0:T(1,128)S(1)}, f32[1,512]{1,0:T(1,128)}, u32[]{:S(2)}) copy-start(f32[1,512]{1,0:T(1,128)} %get-tuple-element.847) | copy-start | bytes 6148 | tf_op jit(solution)/shard_map/while
  104.8 6.7 %collective-permute-start.8 = (bf16[1,32,512]{2,1,0:T(8,128)(2,1)S(1)}, bf16[1,32,512]{2,1,0:T(8,128)(2,1)S(1)}, u32[]{:S(2)}, u32[]{:S(2)}) collective-permute-start(bf16[1,32,512]{2,1,0:T(8,128)(2,1)S(1)} %convert_element_type.109), channel_id=1, source_target_pairs={{0,4},{4,8},{8,12},{12,16},{16,20},{20,24},{24,28},{28,0},{1,5},{5... | collective-permute-start | bytes 98312 | tf_op jit(solution)/shard_map/ppermute | solution.py:17
  104.9 6.6 %collective-permute-start.7 = (bf16[1,32,512]{2,1,0:T(8,128)(2,1)S(1)}, bf16[1,32,512]{2,1,0:T(8,128)(2,1)S(1)}, u32[]{:S(2)}, u32[]{:S(2)}) collective-permute-start(bf16[1,32,512]{2,1,0:T(8,128)(2,1)S(1)} %convert_element_type.109), channel_id=1, source_target_pairs={{0,28},{4,0},{8,4},{12,8},{16,12},{20,16},{24,20},{28,24},{1,29},{... | collective-permute-start | bytes 98312 | tf_op jit(solution)/shard_map/ppermute | solution.py:19
  111.5 6.6 %collective-permute-start.10 = (bf16[1,32,512]{2,1,0:T(8,128)(2,1)S(1)}, bf16[1,32,512]{2,1,0:T(8,128)(2,1)S(1)}, u32[]{:S(2)}, u32[]{:S(2)}) collective-permute-start(bf16[1,32,512]{2,1,0:T(8,128)(2,1)S(1)} %collective-permute-done.8), channel_id=1, source_target_pairs={{0,4},{4,8},{8,12},{12,16},{16,20},{20,24},{24,28},{28,0},{1,5},{5... | collective-permute-start | bytes 98312 | tf_op jit(solution)/shard_map/ppermute | solution.py:17
  111.5 6.6 %collective-permute-start.9 = (bf16[1,32,512]{2,1,0:T(8,128)(2,1)S(1)}, bf16[1,32,512]{2,1,0:T(8,128)(2,1)S(1)}, u32[]{:S(2)}, u32[]{:S(2)}) collective-permute-start(bf16[1,32,512]{2,1,0:T(8,128)(2,1)S(1)} %collective-permute-done.7), channel_id=1, source_target_pairs={{0,28},{4,0},{8,4},{12,8},{16,12},{20,16},{24,20},{28,24},{1,29},{... | collective-permute-start | bytes 98312 | tf_op jit(solution)/shard_map/ppermute | solution.py:19
  118.1 6.6 %collective-permute-start.12 = (bf16[1,32,512]{2,1,0:T(8,128)(2,1)S(1)}, bf16[1,32,512]{2,1,0:T(8,128)(2,1)S(1)}, u32[]{:S(2)}, u32[]{:S(2)}) collective-permute-start(bf16[1,32,512]{2,1,0:T(8,128)(2,1)S(1)} %collective-permute-done.10), channel_id=1, source_target_pairs={{0,4},{4,8},{8,12},{12,16},{16,20},{20,24},{24,28},{28,0},{1,5},{5... | collective-permute-start | bytes 98312 | tf_op jit(solution)/shard_map/ppermute | solution.py:17
  118.1 6.7 %collective-permute-start.11 = (bf16[1,32,512]{2,1,0:T(8,128)(2,1)S(1)}, bf16[1,32,512]{2,1,0:T(8,128)(2,1)S(1)}, u32[]{:S(2)}, u32[]{:S(2)}) collective-permute-start(bf16[1,32,512]{2,1,0:T(8,128)(2,1)S(1)} %collective-permute-done.9), channel_id=1, source_target_pairs={{0,28},{4,0},{8,4},{12,8},{16,12},{20,16},{24,20},{28,24},{1,29},{... | collective-permute-start | bytes 98312 | tf_op jit(solution)/shard_map/ppermute | solution.py:19
  124.7 6.6 %collective-permute-start.13 = (bf16[1,32,512]{2,1,0:T(8,128)(2,1)S(1)}, bf16[1,32,512]{2,1,0:T(8,128)(2,1)S(1)}, u32[]{:S(2)}, u32[]{:S(2)}) collective-permute-start(bf16[1,32,512]{2,1,0:T(8,128)(2,1)S(1)} %collective-permute-done.12), channel_id=1, source_target_pairs={{0,4},{4,8},{8,12},{12,16},{16,20},{20,24},{24,28},{28,0},{1,5},{5... | collective-permute-start | bytes 98312 | tf_op jit(solution)/shard_map/ppermute | solution.py:17
  131.6 8.5 %copy-start.1 = (bf16[1,2048,512]{2,1,0:T(8,128)(2,1)S(1)}, bf16[1,2048,512]{2,1,0:T(8,128)(2,1)}, u32[]{:S(2)}) copy-start(bf16[1,2048,512]{2,1,0:T(8,128)(2,1)} %get-tuple-element.895) | copy-start | bytes 6291460 | tf_op jit(solution)/shard_map/while
  131.6 8.5 %copy-start.4 = (f32[1,512]{1,0:T(1,128)S(1)}, f32[1,512]{1,0:T(1,128)}, u32[]{:S(2)}) copy-start(f32[1,512]{1,0:T(1,128)} %get-tuple-element.889) | copy-start | bytes 6148 | tf_op jit(solution)/shard_map/while
  140.7 8.6 %copy-start.1 = (bf16[1,2048,512]{2,1,0:T(8,128)(2,1)S(1)}, bf16[1,2048,512]{2,1,0:T(8,128)(2,1)}, u32[]{:S(2)}) copy-start(bf16[1,2048,512]{2,1,0:T(8,128)(2,1)} %get-tuple-element.895) | copy-start | bytes 6291460 | tf_op jit(solution)/shard_map/while
  140.8 8.6 %copy-start.4 = (f32[1,512]{1,0:T(1,128)S(1)}, f32[1,512]{1,0:T(1,128)}, u32[]{:S(2)}) copy-start(f32[1,512]{1,0:T(1,128)} %get-tuple-element.889) | copy-start | bytes 6148 | tf_op jit(solution)/shard_map/while
  150.0 8.6 %copy-start.1 = (bf16[1,2048,512]{2,1,0:T(8,128)(2,1)S(1)}, bf16[1,2048,512]{2,1,0:T(8,128)(2,1)}, u32[]{:S(2)}) copy-start(bf16[1,2048,512]{2,1,0:T(8,128)(2,1)} %get-tuple-element.895) | copy-start | bytes 6291460 | tf_op jit(solution)/shard_map/while
  150.0 8.6 %copy-start.4 = (f32[1,512]{1,0:T(1,128)S(1)}, f32[1,512]{1,0:T(1,128)}, u32[]{:S(2)}) copy-start(f32[1,512]{1,0:T(1,128)} %get-tuple-element.889) | copy-start | bytes 6148 | tf_op jit(solution)/shard_map/while
  159.2 8.6 %copy-start.1 = (bf16[1,2048,512]{2,1,0:T(8,128)(2,1)S(1)}, bf16[1,2048,512]{2,1,0:T(8,128)(2,1)}, u32[]{:S(2)}) copy-start(bf16[1,2048,512]{2,1,0:T(8,128)(2,1)} %get-tuple-element.895) | copy-start | bytes 6291460 | tf_op jit(solution)/shard_map/while
  159.2 8.6 %copy-start.4 = (f32[1,512]{1,0:T(1,128)S(1)}, f32[1,512]{1,0:T(1,128)}, u32[]{:S(2)}) copy-start(f32[1,512]{1,0:T(1,128)} %get-tuple-element.889) | copy-start | bytes 6148 | tf_op jit(solution)/shard_map/while
  168.4 8.6 %copy-start.1 = (bf16[1,2048,512]{2,1,0:T(8,128)(2,1)S(1)}, bf16[1,2048,512]{2,1,0:T(8,128)(2,1)}, u32[]{:S(2)}) copy-start(bf16[1,2048,512]{2,1,0:T(8,128)(2,1)} %get-tuple-element.895) | copy-start | bytes 6291460 | tf_op jit(solution)/shard_map/while
  168.5 8.6 %copy-start.4 = (f32[1,512]{1,0:T(1,128)S(1)}, f32[1,512]{1,0:T(1,128)}, u32[]{:S(2)}) copy-start(f32[1,512]{1,0:T(1,128)} %get-tuple-element.889) | copy-start | bytes 6148 | tf_op jit(solution)/shard_map/while
  177.7 8.6 %copy-start.1 = (bf16[1,2048,512]{2,1,0:T(8,128)(2,1)S(1)}, bf16[1,2048,512]{2,1,0:T(8,128)(2,1)}, u32[]{:S(2)}) copy-start(bf16[1,2048,512]{2,1,0:T(8,128)(2,1)} %get-tuple-element.895) | copy-start | bytes 6291460 | tf_op jit(solution)/shard_map/while
  177.7 8.6 %copy-start.4 = (f32[1,512]{1,0:T(1,128)S(1)}, f32[1,512]{1,0:T(1,128)}, u32[]{:S(2)}) copy-start(f32[1,512]{1,0:T(1,128)} %get-tuple-element.889) | copy-start | bytes 6148 | tf_op jit(solution)/shard_map/while
  186.9 8.6 %copy-start.1 = (bf16[1,2048,512]{2,1,0:T(8,128)(2,1)S(1)}, bf16[1,2048,512]{2,1,0:T(8,128)(2,1)}, u32[]{:S(2)}) copy-start(bf16[1,2048,512]{2,1,0:T(8,128)(2,1)} %get-tuple-element.895) | copy-start | bytes 6291460 | tf_op jit(solution)/shard_map/while
  186.9 8.6 %copy-start.4 = (f32[1,512]{1,0:T(1,128)S(1)}, f32[1,512]{1,0:T(1,128)}, u32[]{:S(2)}) copy-start(f32[1,512]{1,0:T(1,128)} %get-tuple-element.889) | copy-start | bytes 6148 | tf_op jit(solution)/shard_map/while
  196.2 8.6 %copy-start.1 = (bf16[1,2048,512]{2,1,0:T(8,128)(2,1)S(1)}, bf16[1,2048,512]{2,1,0:T(8,128)(2,1)}, u32[]{:S(2)}) copy-start(bf16[1,2048,512]{2,1,0:T(8,128)(2,1)} %get-tuple-element.895) | copy-start | bytes 6291460 | tf_op jit(solution)/shard_map/while
  196.2 8.6 %copy-start.4 = (f32[1,512]{1,0:T(1,128)S(1)}, f32[1,512]{1,0:T(1,128)}, u32[]{:S(2)}) copy-start(f32[1,512]{1,0:T(1,128)} %get-tuple-element.889) | copy-start | bytes 6148 | tf_op jit(solution)/shard_map/while
  205.4 1.0 copy-start.2
